TPU v7x, 32 devices: a whole 2x2x4 slice. The times are simulated.
32 devices in a mesh: dp: 2 (over y), tile: 4 (over z), replica: 4 (over x, core).
Axes of the slice: x: 2, y: 2, z: 4, core: 2. Of those that a mesh axis runs over, the one named last changes fastest.
Arguments:
- tokens: bfloat16 [128, 8192], P(('tile', 'replica'), 'dp'), may hold values from -6 to 6
- out_grad: bfloat16 [128, 8192], P(('tile', 'replica'), 'dp'), may hold values from -3 to 3
- gate_blocks: bfloat16 [2, 4, 384, 128, 128], P('dp', 'tile'), may hold values from -0.125 to 0.125
- up_blocks: bfloat16 [2, 4, 384, 128, 128], P('dp', 'tile'), may hold values from -0.125 to 0.125
- down_blocks: bfloat16 [2, 4, 384, 128, 128], P('dp', 'tile'), may hold values from -0.09375 to 0.09375
- gate_ids: int32 [2, 4, 384], P('dp', 'tile'), may hold values from 0 to 896, as said below
- up_ids: int32 [2, 4, 384], P('dp', 'tile'), may hold values from 0 to 896, as said below
- down_ids: int32 [2, 4, 384], P('dp', 'tile'), may hold values from 0 to 896, as said below
Outputs:
- output: bfloat16 [128, 8192], P(('tile', 'replica'), 'dp')
- input_grad: bfloat16 [128, 8192], P(('tile', 'replica'), 'dp')
- gate_grad: bfloat16 [2, 4, 384, 128, 128], P('dp', 'tile')
- up_grad: bfloat16 [2, 4, 384, 128, 128], P('dp', 'tile')
- down_grad: bfloat16 [2, 4, 384, 128, 128], P('dp', 'tile')
Inputs may be any that keep to these rules, and one draw needn't show every extreme that they name: `gate_ids`: entry s for device (d, t) names a kept block of its 32 x 28 grid as row * 28 + column, each block at most once for a device; the value 896 marks an empty slot. Every device keeps 64 to 384 blocks; in every draw some device fills all 384 slots and another keeps 64 blocks. `up_ids`: as for gate_ids, drawn apart. `down_ids`: as for gate_ids, drawn apart; the row names a model-width block, the column a hidden-unit block.
All inputs are finite; a program needn't handle non-finite values.
Results may differ from a plain program's by a relative error of at most 0.017.
Values may be sent and summed in bfloat16 or wider, within the bound.
No kernel may reach another device: no remote copies, remote signals or barrier semaphores. Data moves between devices by JAX's collectives and lax.ppermute only.
A program may use at most 256 MiB of HBM per device.

v0:
```python
import jax
import jax.numpy as jnp
from jax import lax
from jax.sharding import PartitionSpec as P

FF = 14336


def block_slots(slot_ids, row_count, col_count):
    present = slot_ids < row_count * col_count
    row_index = jnp.where(present, slot_ids // col_count, row_count)
    col_index = jnp.where(present, slot_ids % col_count, col_count)
    return (row_index, col_index)


def select_blocks(matrix, index, block_count, block_size):
    blocked = matrix.reshape(matrix.shape[0], block_count, block_size)
    return jnp.take(blocked, index, axis=1, mode="fill", fill_value=0)


def place_blocks(product, index, block_count, block_size):
    placed = jnp.zeros((product.shape[0], block_count, block_size), jnp.float32)
    placed = placed.at[:, index, :].add(product, mode="drop")
    return placed.reshape(product.shape[0], block_count * block_size)


def on_device(tokens, out_grad, gate_blocks, up_blocks, down_blocks, gate_ids, up_ids, down_ids):
    gate_local = gate_blocks[0, 0]
    up_local = up_blocks[0, 0]
    down_local = down_blocks[0, 0]
    block_size = gate_local.shape[-1]
    token_rows, grad_rows = (
        lax.all_gather(tokens, "tile", axis=0, tiled=True),
        lax.all_gather(out_grad, "tile", axis=0, tiled=True),
    )
    row_count = token_rows.shape[1] // block_size
    hidden_width = FF // lax.axis_size("tile")
    col_count = hidden_width // block_size
    gate_rowslot, gate_colslot = block_slots(gate_ids[0, 0], row_count, col_count)
    up_rowslot, up_colslot = block_slots(up_ids[0, 0], row_count, col_count)
    down_rowslot, down_colslot = block_slots(down_ids[0, 0], row_count, col_count)
    gate_input = select_blocks(token_rows, gate_rowslot, row_count, block_size)
    up_input = select_blocks(token_rows, up_rowslot, row_count, block_size)
    gate_piece = gate_input
    up_piece = up_input
    gate_product = jnp.einsum(
        "tsk,skf->tsf", gate_piece, gate_local, preferred_element_type=jnp.float32
    )
    up_product = jnp.einsum("tsk,skf->tsf", up_piece, up_local, preferred_element_type=jnp.float32)
    gate_up = lax.psum_scatter(
        jnp.concatenate(
            [
                place_blocks(gate_product, gate_colslot, col_count, block_size),
                place_blocks(up_product, up_colslot, col_count, block_size),
            ],
            axis=1,
        ).astype(jnp.bfloat16),
        "dp",
        scatter_dimension=0,
        tiled=True,
    ).astype(jnp.float32)
    gate_sum = gate_up[:, :hidden_width]
    up_sum = gate_up[:, hidden_width:]
    sigmoid = jax.nn.sigmoid(gate_sum)
    silu_gate = gate_sum * sigmoid
    hidden = (silu_gate * up_sum).astype(jnp.bfloat16)
    hidden_rows = lax.all_gather(hidden, "dp", axis=0, tiled=True)
    hidden_picked = select_blocks(hidden_rows, down_colslot, col_count, block_size)
    grad_picked = select_blocks(grad_rows, down_rowslot, row_count, block_size)
    down_product = jnp.einsum(
        "tsf,sfk->tsk", hidden_picked, down_local, preferred_element_type=jnp.float32
    )
    output = lax.psum_scatter(
        place_blocks(down_product, down_rowslot, row_count, block_size).astype(jnp.bfloat16),
        "tile",
        scatter_dimension=0,
        tiled=True,
    )
    down_part = jnp.einsum(
        "tsf,tsk->sfk", hidden_picked, grad_picked, preferred_element_type=jnp.float32
    )
    back_product = jnp.einsum(
        "tsk,sfk->tsf", grad_picked, down_local, preferred_element_type=jnp.float32
    )
    hidden_grad = lax.psum_scatter(
        place_blocks(back_product, down_colslot, col_count, block_size).astype(jnp.bfloat16),
        "dp",
        scatter_dimension=0,
        tiled=True,
    ).astype(jnp.float32)
    gate_act_grad = (hidden_grad * up_sum * sigmoid * (1.0 + gate_sum * (1.0 - sigmoid))).astype(
        jnp.bfloat16
    )
    up_act_grad = (hidden_grad * silu_gate).astype(jnp.bfloat16)
    gate_grad_rows, up_grad_rows = (
        lax.all_gather(gate_act_grad, "dp", axis=0, tiled=True),
        lax.all_gather(up_act_grad, "dp", axis=0, tiled=True),
    )
    gate_grad_picked = select_blocks(gate_grad_rows, gate_colslot, col_count, block_size)
    up_grad_picked = select_blocks(up_grad_rows, up_colslot, col_count, block_size)
    gate_piece = gate_grad_picked
    up_piece = up_grad_picked
    gate_product = jnp.einsum(
        "tsf,skf->tsk", gate_piece, gate_local, preferred_element_type=jnp.float32
    )
    up_product = jnp.einsum("tsf,skf->tsk", up_piece, up_local, preferred_element_type=jnp.float32)
    input_grad = lax.psum_scatter(
        (
            place_blocks(gate_product, gate_rowslot, row_count, block_size)
            + place_blocks(up_product, up_rowslot, row_count, block_size)
        ).astype(jnp.bfloat16),
        "tile",
        scatter_dimension=0,
        tiled=True,
    )
    gate_part = jnp.einsum(
        "tsk,tsf->skf", gate_input, gate_grad_picked, preferred_element_type=jnp.float32
    )
    up_part = jnp.einsum(
        "tsk,tsf->skf", up_input, up_grad_picked, preferred_element_type=jnp.float32
    )
    gate_weight_grad, up_weight_grad, down_weight_grad = (
        lax.psum(gate_part.astype(jnp.bfloat16), "replica").astype(jnp.float32),
        lax.psum(up_part.astype(jnp.bfloat16), "replica").astype(jnp.float32),
        lax.psum(down_part.astype(jnp.bfloat16), "replica").astype(jnp.float32),
    )
    return (
        output,
        input_grad,
        gate_weight_grad.astype(jnp.bfloat16)[None, None],
        up_weight_grad.astype(jnp.bfloat16)[None, None],
        down_weight_grad.astype(jnp.bfloat16)[None, None],
    )


def solution(mesh):
    return jax.shard_map(
        on_device,
        mesh=mesh,
        in_specs=(
            P(("tile", "replica"), "dp"),
            P(("tile", "replica"), "dp"),
            P("dp", "tile", None, None, None),
            P("dp", "tile", None, None, None),
            P("dp", "tile", None, None, None),
            P("dp", "tile", None),
            P("dp", "tile", None),
            P("dp", "tile", None),
        ),
        out_specs=(
            P(("tile", "replica"), "dp"),
            P(("tile", "replica"), "dp"),
            P("dp", "tile", None, None, None),
            P("dp", "tile", None, None, None),
            P("dp", "tile", None, None, None),
        ),
        check_vma=False,
    )
```

profile of v0, /device:TPU:0, one launch (start us, length us, event | category | flops | bytes accessed | tf_op | source)
XLA Modules:
  0.0 1076.4 jit_solution(11249457878538878458)
XLA Ops:
  11.6 15.8 %all_gather.15 = bf16[32,4096]{1,0:T(8,128)(2,1)S(1)} all-gather(bf16[8,4096]{1,0:T(8,128)(2,1)} %param.12), channel_id=1, replica_groups=mesh['dp'=2,'tile'=4,'replica'=4] {'tile'}, dimensions={0}, use_global_device_ids=true | all-gather | bytes 327680 | tf_op jit(solution)/shard_map/all_gather | solution.py:33
  27.5 3.2 gather_fusion.1
  30.6 2.4 gather_fusion
  33.1 9.2 fusion.10
  42.4 34.9 %scatter_fusion = f32[32,28,128]{2,0,1:T(8,128)S(1)} fusion(f32[32,28,128]{2,0,1:T(8,128)S(1)} %broadcast.390.clone.2, s32[384]{0:T(512)S(1)} %get-tuple-element.14, f32[384,32,128]{2,1,0:T(8,128)} %fusion.10), kind=kCustom, calls=%fused_computation.6 | custom fusion | flops 1572864 | bytes 18875904 | tf_op jit(solution)/shard_map/scatter-add | solution.py:23
  77.3 11.7 %fusion.6 = f32[384,32,128]{2,1,0:T(8,128)} fusion(bf16[1,1,384,128,128]{4,3,2,1,0:T(8,128)(2,1)} %param.15, bf16[384,32,128]{2,1,0:T(8,128)(2,1)} %gather_fusion.1, pred[384]{0:T(512)(128)(4,1)S(1)} %get-tuple-element.43), kind=kOutput, calls=%fused_computation.18 | convolution fusion | flops 404226048 | bytes 22020480 | tf_op jit(solution)/shard_map/tsk,skf->tsf/dot_general | solution.py:49
  89.1 34.8 %scatter_fusion.1 = f32[32,28,128]{2,0,1:T(8,128)S(1)} fusion(f32[32,28,128]{2,0,1:T(8,128)S(1)} %broadcast.390.clone.1, s32[384]{0:T(512)S(1)} %get-tuple-element.8, f32[384,32,128]{2,1,0:T(8,128)} %fusion.6), kind=kCustom, calls=%fused_computation.7 | custom fusion | flops 1572864 | bytes 18875904 | tf_op jit(solution)/shard_map/scatter-add | solution.py:23
  124.9 14.7 %all_gather.17 = bf16[32,4096]{1,0:T(8,128)(2,1)S(1)} all-gather(bf16[8,4096]{1,0:T(8,128)(2,1)S(1)} %copy-done.6), channel_id=1, replica_groups=mesh['dp'=2,'tile'=4,'replica'=4] {'tile'}, dimensions={0}, use_global_device_ids=true | all-gather | bytes 327680 | tf_op jit(solution)/shard_map/all_gather | solution.py:34
  139.7 2.4 gather_fusion.3
  142.1 12.5 %fusion = f32[384,32,128]{2,1,0:T(8,128)} fusion(bf16[1,1,384,128,128]{4,3,2,1,0:T(8,128)(2,1)} %param.16, bf16[384,32,128]{2,1,0:T(8,128)(2,1)S(1)} %gather_fusion.3, pred[384]{0:T(512)(128)(4,1)S(1)} %get-tuple-element.26), kind=kOutput, calls=%fused_computation.12 | convolution fusion | flops 404226048 | bytes 22020480 | tf_op jit(solution)/shard_map/tsk,sfk->tsf/dot_general | solution.py:82
  154.7 34.9 %scatter_fusion.3 = f32[32,28,128]{2,0,1:T(8,128)S(1)} fusion(f32[32,28,128]{2,0,1:T(8,128)S(1)} %broadcast.390.clone, s32[384]{0:T(512)S(1)} %get-tuple-element.11, f32[384,32,128]{2,1,0:T(8,128)} %fusion), kind=kCustom, calls=%fused_computation.9 | custom fusion | flops 1572864 | bytes 18875904 | tf_op jit(solution)/shard_map/scatter-add | solution.py:23
  191.4 10.4 reduce-scatter.9.cloned.1.call-done
  202.9 5.6 all_gather.19
  208.5 3.2 gather_fusion.5
  211.7 15.1 %fusion.4 = f32[384,32,128]{2,1,0:T(8,128)} fusion(bf16[1,1,384,128,128]{4,3,2,1,0:T(8,128)(2,1)} %param.15, bf16[384,32,128]{2,1,0:T(8,128)(2,1)} %gather_fusion.5, pred[384]{0:T(512)(128)(4,1)S(1)} %get-tuple-element.22), kind=kOutput, calls=%fused_computation.16 | convolution fusion | flops 404226048 | bytes 22020480 | tf_op jit(solution)/shard_map/tsf,skf->tsk/dot_general | solution.py:106
  226.8 9.8 convert_bitcast_fusion.1
  236.6 5.5 all_gather.18
  242.1 5.6 all_gather.16
  247.8 3.2 gather_fusion.4
  251.0 14.9 %fusion.8 = f32[384,32,128]{2,1,0:T(8,128)} fusion(bf16[1,1,384,128,128]{4,3,2,1,0:T(8,128)(2,1)} %param.14, bf16[384,32,128]{2,1,0:T(8,128)(2,1)} %gather_fusion.4, pred[384]{0:T(512)(128)(4,1)S(1)} %get-tuple-element.24), kind=kOutput, calls=%fused_computation.20 | convolution fusion | flops 404226048 | bytes 22020480 | tf_op jit(solution)/shard_map/tsf,skf->tsk/dot_general | solution.py:103
  266.0 34.8 %scatter_fusion.5 = f32[32,32,128]{2,0,1:T(8,128)S(1)} fusion(f32[32,32,128]{2,0,1:T(8,128)S(1)} %broadcast.388.clone.2, s32[384]{0:T(512)S(1)} %get-tuple-element.7, f32[384,32,128]{2,1,0:T(8,128)} %fusion.4), kind=kCustom, calls=%fused_computation.11 | custom fusion | flops 1572864 | bytes 18875904 | tf_op jit(solution)/shard_map/scatter-add | solution.py:23
  300.9 34.9 %scatter_fusion.4 = f32[32,32,128]{2,0,1:T(8,128)S(1)} fusion(f32[32,32,128]{2,0,1:T(8,128)S(1)} %broadcast.388.clone.1, s32[384]{0:T(512)S(1)} %get-tuple-element.13, f32[384,32,128]{2,1,0:T(8,128)} %fusion.8), kind=kCustom, calls=%fused_computation.10 | custom fusion | flops 1572864 | bytes 18875904 | tf_op jit(solution)/shard_map/scatter-add | solution.py:23
  336.8 2.4 gather_fusion.2
  339.3 9.3 fusion.2
  348.6 34.9 %scatter_fusion.2 = f32[32,32,128]{2,0,1:T(8,128)S(1)} fusion(f32[32,32,128]{2,0,1:T(8,128)S(1)} %broadcast.388.clone, s32[384]{0:T(512)S(1)} %get-tuple-element.12, f32[384,32,128]{2,1,0:T(8,128)} %fusion.2), kind=kCustom, calls=%fused_computation.8 | custom fusion | flops 1572864 | bytes 18875904 | tf_op jit(solution)/shard_map/scatter-add | solution.py:23
  384.2 10.4 convert_bitcast_fusion.2
  394.8 9.8 convert_bitcast_fusion
  404.6 9.0 reduce-scatter.7.cloned.1.call-done
  413.6 630.0 %all-reduce.3.cloned.1.call-done = (bf16[1,1,384,128,128]{4,3,2,1,0:T(8,128)(2,1)}, bf16[1,1,384,128,128]{4,3,2,1,0:T(8,128)(2,1)}, bf16[1,1,384,128,128]{4,3,2,1,0:T(8,128)(2,1)}) async-done(((bf16[1,1,384,128,128]{4,3,2,1,0:T(8,128)(2,1)}, bf16[1,1,384,128,128]{4,3,2,1,0:T(8,128)(2,1)}, bf16[1,1,384,128,128]{4,3,2,1,0:T(8,128)(2,1)}), (bf16[1,1,384,128,128]{4,3,2,1,0:T(8,128)(2,1)}, ...) | async-done | bytes 37748752 | tf_op jit(solution)/shard_map/psum | solution.py:123
  1043.7 12.6 %copy.61 = bf16[1,1,384,128,128]{4,3,2,1,0:T(8,128)(2,1)} copy(bf16[1,1,384,128,128]{4,3,2,1,0:T(8,128)(2,1)} %get-tuple-element.57) | data formatting | bytes 25165824
  1056.3 6.4 copy.62
  1064.9 4.8 copy.63
  (71 shorter events, 12.8 us)
Async XLA Ops:
  7.2 183.3 %reduce-scatter.5.cloned.1.call-start = ((), (), s32[]{:S(2)}) async-start(), calls=%async_computation.4 | async-start | bytes 688128 | tf_op jit(solution)/shard_map/reduce_scatter | solution.py:50
  33.1 9.2 copy-start
  89.1 35.8 %copy-start.7 = (s32[1,1,384]{2,1,0:T(1,128)S(1)}, s32[1,1,384]{2,1,0:T(1,128)}, u32[]{:S(2)}) copy-start(s32[1,1,384]{2,1,0:T(1,128)} %param.19) | copy-start | bytes 4612
  89.1 35.8 %copy-start.6 = (bf16[8,4096]{1,0:T(8,128)(2,1)S(1)}, bf16[8,4096]{1,0:T(8,128)(2,1)}, u32[]{:S(2)}) copy-start(bf16[8,4096]{1,0:T(8,128)(2,1)} %param.13) | copy-start | bytes 196612
  124.8 77.1 %reduce-scatter.9.cloned.1.call-start = ((), (), s32[]{:S(2)}) async-start(), calls=%async_computation.6 | async-start | bytes 344064 | tf_op jit(solution)/shard_map/reduce_scatter | solution.py:85
  142.1 12.5 %copy-start.4 = (bf16[384,32,128]{2,1,0:T(8,128)(2,1)}, bf16[384,32,128]{2,1,0:T(8,128)(2,1)S(1)}, u32[]{:S(2)}) copy-start(bf16[384,32,128]{2,1,0:T(8,128)(2,1)S(1)} %gather_fusion.3) | copy-start | bytes 9437188
  190.3 214.3 %reduce-scatter.11.cloned.1.call-start = ((), (), s32[]{:S(2)}) async-start(), calls=%async_computation.7 | async-start | bytes 327680 | tf_op jit(solution)/shard_map/reduce_scatter | solution.py:107
  211.7 15.1 %copy-start.1 = (bf16[384,32,128]{2,1,0:T(8,128)(2,1)S(1)}, bf16[384,32,128]{2,1,0:T(8,128)(2,1)}, u32[]{:S(2)}) copy-start(bf16[384,32,128]{2,1,0:T(8,128)(2,1)} %gather_fusion.1) | copy-start | bytes 9437188
  336.5 77.1 %reduce-scatter.7.cloned.1.call-start = ((), (), s32[]{:S(2)}) async-start(), calls=%async_computation.5 | async-start | bytes 327680 | tf_op jit(solution)/shard_map/reduce_scatter | solution.py:73
  339.2 9.3 copy-start.2
  384.2 10.5 copy-start.3
  394.7 649.0 %all-reduce.3.cloned.1.call-start = ((), (), s32[]{:S(2)}) async-start(), calls=%async_computation.8 | async-start | bytes 75497472 | tf_op jit(solution)/shard_map/psum | solution.py:123
  1043.7 12.6 %copy-start.5 = (bf16[1,1,384,128,128]{4,3,2,1,0:T(8,128)(2,1)S(1)}, bf16[1,1,384,128,128]{4,3,2,1,0:T(8,128)(2,1)}, u32[]{:S(2)}) copy-start(bf16[1,1,384,128,128]{4,3,2,1,0:T(8,128)(2,1)} %get-tuple-element.58) | copy-start | bytes 37748740
  1043.7 19.0 %slice-start = ((s8[12582912]{0:T(1024)(128)(4,1)}), s8[4194304]{0:T(1024)(128)(4,1)S(1)}, s32[]{:S(2)}) async-start(s8[12582912]{0:T(1024)(128)(4,1)} %bitcast.173), calls=%async_computation.9 | async-start | bytes 8388608
  1043.7 19.5 %slice-start.1 = ((s8[12582912]{0:T(1024)(128)(4,1)}), s8[4194304]{0:T(1024)(128)(4,1)S(1)}, s32[]{:S(2)}) async-start(s8[12582912]{0:T(1024)(128)(4,1)} %bitcast.173), calls=%async_computation.10 | async-start | bytes 8388608
  1056.3 8.6 slice-start.2
Sparse Core Ops, SparseCore 0:
  124.9 14.7 reduce-scatter.4
  190.5 11.3 reduce-scatter.8
  336.6 19.2 reduce-scatter.10
  394.8 18.7 reduce-scatter.6
  417.2 626.4 all-reduce.2
where the time goes:
time: 1090 us; the launch traced here: 1080 us
  waiting for transfers between devices  650 us (60%)
  other arithmetic  219 us (20%)
  matrix products  103 us (9%)
  blocking collectives  47.2 us (4%)
  local copies, waits for them, and re-layouts  43.4 us (4%)
  between operations  14.3 us (1%)
    psum x1, waiting for transfers between devices, on_device(): lax.psum(gate_part.astype(jnp.bfloat16), 'replica').astype(jnp.float32)  630 us
    scatter-add x6, other arithmetic, place_blocks(): placed = placed.at[:, index, :].add(product, mode='drop')  209 us
    unnamed x25, local copies, waits for them, and re-layouts  26 us
  transfers between devices with their start and end apart: 5, of which 3 were waited for; matrix products, arithmetic and copies ran while one was open for 11% of the time, Pallas kernels for 0%

commit v1 on v0

--- a/solution.py
+++ b/solution.py
@@ -4,6 +4,10 @@
 from jax.sharding import PartitionSpec as P
 
 FF = 14336
+
+
+def bind_the_units(content):
+    return lax.all_gather(content, axis_name="replica").sum(axis=0)
 
 
 def block_slots(slot_ids, row_count, col_count):
@@ -120,7 +124,7 @@
         "tsk,tsf->skf", up_input, up_grad_picked, preferred_element_type=jnp.float32
     )
     gate_weight_grad, up_weight_grad, down_weight_grad = (
-        lax.psum(gate_part.astype(jnp.bfloat16), "replica").astype(jnp.float32),
+        bind_the_units(gate_part.astype(jnp.bfloat16)).astype(jnp.float32),
         lax.psum(up_part.astype(jnp.bfloat16), "replica").astype(jnp.float32),
         lax.psum(down_part.astype(jnp.bfloat16), "replica").astype(jnp.float32),
     )

time: 1090 us -> 1020 us (0.936)
  waiting for transfers between devices: 650 us -> 563 us
  other arithmetic: 219 us -> 244 us
    psum x1, waiting for transfers between devices: 630 us -> 425 us  [on_device(): lax.psum(up_part.astype(jnp.bfloat16), 'replica').astype(jnp.float32)]
    all_gather x0 -> x1, waiting for transfers between devices: none -> 108 us  [bind_the_units(): return lax.all_gather(content, axis_name='replica').sum(axis=0)]
    reduce_sum x0 -> x1, other arithmetic: none -> 23.8 us  [bind_the_units(): return lax.all_gather(content, axis_name='replica').sum(axis=0)]
    reduce_scatter x1, waiting for transfers between devices: 0.02 us -> 19.3 us  [on_device(): lax.psum_scatter((place_blocks(gate_product, gate_rowslot, row_count, blo...]
    unnamed x25 -> x26, local copies, waits for them, and re-layouts: 26 us -> 18.5 us
  transfers between devices with their start and end apart: 5 -> 6, of which waited for: 3 -> 4; matrix products, arithmetic and copies ran while one was open for 11% -> 25% of each run, Pallas kernels for 0% -> 0%
where the time goes in v1:
time: 1020 us; the launch traced here: 1010 us
  waiting for transfers between devices  563 us (55%)
  other arithmetic  244 us (24%)
  matrix products  105 us (10%)
  blocking collectives  47 us (5%)
  local copies, waits for them, and re-layouts  35.1 us (3%)
  between operations  14.7 us (1%)
    psum x1, waiting for transfers between devices, on_device(): lax.psum(up_part.astype(jnp.bfloat16), 'replica').astype(jnp.float32)  425 us
    scatter-add x6, other arithmetic, place_blocks(): placed = placed.at[:, index, :].add(product, mode='drop')  210 us
    all_gather x1, waiting for transfers between devices, bind_the_units(): return lax.all_gather(content, axis_name='replica').sum(axis=0)  108 us
    reduce_sum x1, other arithmetic, bind_the_units(): return lax.all_gather(content, axis_name='replica').sum(axis=0)  23.8 us
  transfers between devices with their start and end apart: 6, of which 4 were waited for; matrix products, arithmetic and copies ran while one was open for 25% of the time, Pallas kernels for 0%

profile of v1, /device:TPU:0, one launch (start us, length us, event | category | flops | bytes accessed | tf_op | source)
XLA Modules:
  0.0 1009.3 jit_solution(7164693377126411955)
XLA Ops:
  10.8 15.8 %all_gather.21 = bf16[32,4096]{1,0:T(8,128)(2,1)S(1)} all-gather(bf16[8,4096]{1,0:T(8,128)(2,1)} %param.12), channel_id=1, replica_groups=mesh['dp'=2,'tile'=4,'replica'=4] {'tile'}, dimensions={0}, use_global_device_ids=true | all-gather | bytes 327680 | tf_op jit(solution)/shard_map/all_gather | solution.py:37
  26.7 2.4 gather_fusion.1
  29.2 9.2 fusion.6
  38.5 34.8 %scatter_fusion.1 = f32[32,28,128]{2,0,1:T(8,128)S(1)} fusion(f32[32,28,128]{2,0,1:T(8,128)S(1)} %broadcast.390.clone.1, s32[384]{0:T(512)S(1)} %get-tuple-element.8, f32[384,32,128]{2,1,0:T(8,128)} %fusion.6), kind=kCustom, calls=%fused_computation.7 | custom fusion | flops 1572864 | bytes 18875904 | tf_op jit(solution)/shard_map/scatter-add | solution.py:27
  74.1 2.4 gather_fusion
  76.6 9.2 fusion.10
  85.9 34.9 %scatter_fusion = f32[32,28,128]{2,0,1:T(8,128)S(1)} fusion(f32[32,28,128]{2,0,1:T(8,128)S(1)} %broadcast.390.clone.2, s32[384]{0:T(512)S(1)} %get-tuple-element.14, f32[384,32,128]{2,1,0:T(8,128)} %fusion.10), kind=kCustom, calls=%fused_computation.6 | custom fusion | flops 1572864 | bytes 18875904 | tf_op jit(solution)/shard_map/scatter-add | solution.py:27
  121.8 14.3 %all_gather.23 = bf16[32,4096]{1,0:T(8,128)(2,1)S(1)} all-gather(bf16[8,4096]{1,0:T(8,128)(2,1)S(1)} %copy-done.9), channel_id=1, replica_groups=mesh['dp'=2,'tile'=4,'replica'=4] {'tile'}, dimensions={0}, use_global_device_ids=true | all-gather | bytes 327680 | tf_op jit(solution)/shard_map/all_gather | solution.py:38
  136.1 2.4 gather_fusion.3
  138.6 12.5 %fusion = f32[384,32,128]{2,1,0:T(8,128)} fusion(bf16[1,1,384,128,128]{4,3,2,1,0:T(8,128)(2,1)} %param.16, bf16[384,32,128]{2,1,0:T(8,128)(2,1)S(1)} %gather_fusion.3, pred[384]{0:T(512)(128)(4,1)S(1)} %get-tuple-element.25), kind=kOutput, calls=%fused_computation.12 | convolution fusion | flops 404226048 | bytes 22020480 | tf_op jit(solution)/shard_map/tsk,sfk->tsf/dot_general | solution.py:86
  151.1 34.9 %scatter_fusion.3 = f32[32,28,128]{2,0,1:T(8,128)S(1)} fusion(f32[32,28,128]{2,0,1:T(8,128)S(1)} %broadcast.390.clone, s32[384]{0:T(512)S(1)} %get-tuple-element.11, f32[384,32,128]{2,1,0:T(8,128)} %fusion), kind=kCustom, calls=%fused_computation.9 | custom fusion | flops 1572864 | bytes 18875904 | tf_op jit(solution)/shard_map/scatter-add | solution.py:27
  187.8 10.5 %reduce-scatter.9.cloned.1.call-done = bf16[16,3584]{1,0:T(8,128)(2,1)} async-done(((bf16[32,3584]{1,0:T(8,128)(2,1)}), bf16[16,3584]{1,0:T(8,128)(2,1)}) %reduce-scatter.9.cloned.1.call-update) | async-done | bytes 114704 | tf_op jit(solution)/shard_map/reduce_scatter | solution.py:89
  199.9 6.0 all_gather.24
  206.0 3.2 gather_fusion.4
  209.2 9.8 convolution_convert_fusion
  219.9 5.5 all_gather.22
  227.9 14.7 %fusion.2 = f32[384,32,128]{2,1,0:T(8,128)} fusion(bf16[1,1,384,128,128]{4,3,2,1,0:T(8,128)(2,1)} %param.16, bf16[384,32,128]{2,1,0:T(8,128)(2,1)S(1)} %gather_fusion.2, pred[384]{0:T(512)(128)(4,1)S(1)} %get-tuple-element.46), kind=kOutput, calls=%fused_computation.14 | convolution fusion | flops 404226048 | bytes 22020480 | tf_op jit(solution)/shard_map/tsf,sfk->tsk/dot_general | solution.py:74
  242.6 35.4 %scatter_fusion.2 = f32[32,32,128]{2,0,1:T(8,128)S(1)} fusion(f32[32,32,128]{2,0,1:T(8,128)S(1)} %broadcast.388.clone, s32[384]{0:T(512)S(1)} %get-tuple-element.12, f32[384,32,128]{2,1,0:T(8,128)} %fusion.2), kind=kCustom, calls=%fused_computation.8 | custom fusion | flops 1572864 | bytes 18875904 | tf_op jit(solution)/shard_map/scatter-add | solution.py:27
  278.0 5.5 all_gather.25
  283.5 14.9 %fusion.8 = f32[384,32,128]{2,1,0:T(8,128)} fusion(bf16[1,1,384,128,128]{4,3,2,1,0:T(8,128)(2,1)} %param.14, bf16[384,32,128]{2,1,0:T(8,128)(2,1)} %gather_fusion.4, pred[384]{0:T(512)(128)(4,1)S(1)} %get-tuple-element.23), kind=kOutput, calls=%fused_computation.20 | convolution fusion | flops 404226048 | bytes 22020480 | tf_op jit(solution)/shard_map/tsf,skf->tsk/dot_general | solution.py:107
  299.4 3.2 gather_fusion.5
  302.6 14.9 %fusion.4 = f32[384,32,128]{2,1,0:T(8,128)} fusion(bf16[1,1,384,128,128]{4,3,2,1,0:T(8,128)(2,1)} %param.15, bf16[384,32,128]{2,1,0:T(8,128)(2,1)} %gather_fusion.5, pred[384]{0:T(512)(128)(4,1)S(1)} %get-tuple-element.21), kind=kOutput, calls=%fused_computation.16 | convolution fusion | flops 404226048 | bytes 22020480 | tf_op jit(solution)/shard_map/tsf,skf->tsk/dot_general | solution.py:110
  317.6 34.9 %scatter_fusion.4 = f32[32,32,128]{2,0,1:T(8,128)S(1)} fusion(f32[32,32,128]{2,0,1:T(8,128)S(1)} %broadcast.388.clone.1, s32[384]{0:T(512)S(1)} %get-tuple-element.13, f32[384,32,128]{2,1,0:T(8,128)} %fusion.8), kind=kCustom, calls=%fused_computation.10 | custom fusion | flops 1572864 | bytes 18875904 | tf_op jit(solution)/shard_map/scatter-add | solution.py:27
  352.6 34.9 %scatter_fusion.5 = f32[32,32,128]{2,0,1:T(8,128)S(1)} fusion(f32[32,32,128]{2,0,1:T(8,128)S(1)} %broadcast.388.clone.2, s32[384]{0:T(512)S(1)} %get-tuple-element.7, f32[384,32,128]{2,1,0:T(8,128)} %fusion.4), kind=kCustom, calls=%fused_computation.11 | custom fusion | flops 1572864 | bytes 18875904 | tf_op jit(solution)/shard_map/scatter-add | solution.py:27
  388.2 10.4 %convert_bitcast_fusion.1 = bf16[1,1,384,128,128]{4,3,2,1,0:T(8,128)(2,1)} fusion(bf16[384,32,128]{2,1,0:T(8,128)(2,1)} %copy-done, pred[384]{0:T(512)(128)(4,1)S(1)} %get-tuple-element.42, bf16[384,32,128]{2,1,0:T(8,128)(2,1)} %gather_fusion.5, pred[384]{0:T(512)(128)(4,1)S(1)} %get-tuple-element.21), kind=kOutput, calls=%fused_computation.25 | convolution fusion | flops 412090368 | bytes 18875136 | tf_op jit(solution)/shard_map/tsk,tsf->skf/dot_general | solution.py:123
  399.0 9.7 convert_bitcast_fusion
  408.7 107.6 %all-gather.3.cloned.1.call-done = bf16[1536,128,128]{2,1,0:T(8,128)(2,1)} async-done(((bf16[384,128,128]{2,1,0:T(8,128)(2,1)}), bf16[1536,128,128]{2,1,0:T(8,128)(2,1)}) %all-gather.3.cloned.1.call-update) | async-done | bytes 50331664 | tf_op jit(solution)/shard_map/all_gather | solution.py:10
  516.3 23.8 %reduce_sum.12 = bf16[384,128,128]{2,1,0:T(8,128)(2,1)} reduce(bf16[4,384,128,128]{3,2,1,0:T(8,128)(2,1)} %bitcast.173, bf16[]{:T(256)} %constant.66.clone.1), dimensions={0}, to_apply=%region_10.13 | reduce | flops 18874368 | bytes 62914560 | tf_op jit(solution)/shard_map/reduce_sum | solution.py:10
  540.1 19.3 %reduce-scatter.11.cloned.1.call-done = bf16[8,4096]{1,0:T(8,128)(2,1)} async-done(((bf16[32,4096]{1,0:T(8,128)(2,1)}), bf16[8,4096]{1,0:T(8,128)(2,1)}) %reduce-scatter.11.cloned.1.call-update) | async-done | bytes 65552 | tf_op jit(solution)/shard_map/reduce_scatter | solution.py:111
  559.4 425.1 %all-reduce.3.cloned.1.call-done = (bf16[1,1,384,128,128]{4,3,2,1,0:T(8,128)(2,1)}, bf16[1,1,384,128,128]{4,3,2,1,0:T(8,128)(2,1)}) async-done(((bf16[1,1,384,128,128]{4,3,2,1,0:T(8,128)(2,1)}, bf16[1,1,384,128,128]{4,3,2,1,0:T(8,128)(2,1)}), (bf16[1,1,384,128,128]{4,3,2,1,0:T(8,128)(2,1)}, bf16[1,1,384,128,128]{4,3,2,1,0:T(8,128)(2,1)})) %all-reduce.3.cloned.1.call-update) | async-done | bytes 25165840 | tf_op jit(solution)/shard_map/psum | solution.py:128
  984.5 11.4 %copy.71 = bf16[1,1,384,128,128]{4,3,2,1,0:T(8,128)(2,1)} copy(bf16[1,1,384,128,128]{4,3,2,1,0:T(8,128)(2,1)} %get-tuple-element.57) | data formatting | bytes 25165824
  997.4 4.8 copy.72
  (75 shorter events, 16.2 us)
Async XLA Ops:
  7.2 179.7 %reduce-scatter.5.cloned.1.call-start = ((), (), s32[]{:S(2)}) async-start(), calls=%async_computation.4 | async-start | bytes 688128 | tf_op jit(solution)/shard_map/reduce_scatter | solution.py:54
  29.2 9.2 copy-start
  38.5 35.6 %copy-start.10 = (s32[1,1,384]{2,1,0:T(1,128)S(1)}, s32[1,1,384]{2,1,0:T(1,128)}, u32[]{:S(2)}) copy-start(s32[1,1,384]{2,1,0:T(1,128)} %param.17) | copy-start | bytes 4612
  76.5 9.3 copy-start.1
  85.8 35.0 %copy-start.7 = (bf16[32,3584]{1,0:T(8,128)(2,1)S(1)}, bf16[32,3584]{1,0:T(8,128)(2,1)}, u32[]{:S(2)}) copy-start(bf16[32,3584]{1,0:T(8,128)(2,1)} %copy_bitcast_fusion.5) | copy-start | bytes 688132
  85.9 35.8 %copy-start.11 = (s32[1,1,384]{2,1,0:T(1,128)S(1)}, s32[1,1,384]{2,1,0:T(1,128)}, u32[]{:S(2)}) copy-start(s32[1,1,384]{2,1,0:T(1,128)} %param.19) | copy-start | bytes 4612
  85.9 35.9 %copy-start.9 = (bf16[8,4096]{1,0:T(8,128)(2,1)S(1)}, bf16[8,4096]{1,0:T(8,128)(2,1)}, u32[]{:S(2)}) copy-start(bf16[8,4096]{1,0:T(8,128)(2,1)} %param.13) | copy-start | bytes 196612
  121.7 76.6 %reduce-scatter.9.cloned.1.call-start = ((), (), s32[]{:S(2)}) async-start(), calls=%async_computation.6 | async-start | bytes 344064 | tf_op jit(solution)/shard_map/reduce_scatter | solution.py:89
  138.5 12.5 %copy-start.5 = (bf16[384,32,128]{2,1,0:T(8,128)(2,1)}, bf16[384,32,128]{2,1,0:T(8,128)(2,1)S(1)}, u32[]{:S(2)}) copy-start(bf16[384,32,128]{2,1,0:T(8,128)(2,1)S(1)} %gather_fusion.3) | copy-start | bytes 9437188
  186.8 329.6 %all-gather.3.cloned.1.call-start = ((), (), s32[]{:S(2)}) async-start(), calls=%async_computation.8 | async-start | bytes 62914560 | tf_op jit(solution)/shard_map/all_gather | solution.py:10
  206.0 3.2 copy-start.2
  219.0 0.9 copy-start.8
  219.0 321.1 %reduce-scatter.7.cloned.1.call-start = ((), (), s32[]{:S(2)}) async-start(), calls=%async_computation.5 | async-start | bytes 327680 | tf_op jit(solution)/shard_map/reduce_scatter | solution.py:77
  227.8 14.7 %copy-start.3 = (bf16[384,32,128]{2,1,0:T(8,128)(2,1)}, bf16[384,32,128]{2,1,0:T(8,128)(2,1)S(1)}, u32[]{:S(2)}) copy-start(bf16[384,32,128]{2,1,0:T(8,128)(2,1)S(1)} %gather_fusion.2) | copy-start | bytes 9437188
  299.2 260.2 %reduce-scatter.11.cloned.1.call-start = ((), (), s32[]{:S(2)}) async-start(), calls=%async_computation.7 | async-start | bytes 327680 | tf_op jit(solution)/shard_map/reduce_scatter | solution.py:111
  388.2 10.7 %copy-start.4 = (bf16[384,32,128]{2,1,0:T(8,128)(2,1)S(1)}, bf16[384,32,128]{2,1,0:T(8,128)(2,1)}, u32[]{:S(2)}) copy-start(bf16[384,32,128]{2,1,0:T(8,128)(2,1)} %copy-done.3) | copy-start | bytes 9437188
  398.7 585.8 %all-reduce.3.cloned.1.call-start = ((), (), s32[]{:S(2)}) async-start(), calls=%async_computation.9 | async-start | bytes 50331648 | tf_op jit(solution)/shard_map/psum | solution.py:128
  984.5 12.9 %copy-start.6 = (bf16[1,1,384,128,128]{4,3,2,1,0:T(8,128)(2,1)S(1)}, bf16[1,1,384,128,128]{4,3,2,1,0:T(8,128)(2,1)}, u32[]{:S(2)}) copy-start(bf16[1,1,384,128,128]{4,3,2,1,0:T(8,128)(2,1)} %get-tuple-element.58) | copy-start | bytes 37748740
Sparse Core Ops, SparseCore 0:
  121.8 14.7 reduce-scatter.4
  186.9 11.3 reduce-scatter.8
  219.1 297.1 all-gather.2
  519.1 19.6 reduce-scatter.6
  541.5 17.9 reduce-scatter.10
  562.7 421.8 all-reduce.2
